TPU v7x, 256 devices: a whole 4x4x8 slice. The times are simulated.
256 devices in a mesh: dp: 8 (over z_hi, x), space: 32 (over z_lo, y, core).
Axes of the slice: x: 4, y: 4, z: 8 (z_hi: 2, z_lo: 4; z = z_hi * 4 + z_lo), core: 2. Of those that a mesh axis runs over, the one named last changes fastest.
Arguments:
- crop: bfloat16 [8, 4, 128, 64, 64], P('dp', None, 'space'), may hold values from -6 to 6
- filter_one: bfloat16 [3, 3, 3, 4, 32], replicated, may hold values from -0.625 to 0.625
- filter_two: bfloat16 [3, 3, 3, 32, 64], replicated, may hold values from -0.21875 to 0.21875
- cotangent: bfloat16 [8, 64, 32, 16, 16], P('dp', None, 'space'), may hold values from -1 to 1
Outputs:
- features: bfloat16 [8, 64, 32, 16, 16], P('dp', None, 'space')
- grad_one: float32 [3, 3, 3, 4, 32], replicated
- grad_two: float32 [3, 3, 3, 32, 64], replicated
All inputs are finite; a program needn't handle non-finite values.
Results may differ from a plain program's by a relative error of at most 0.0045.
The roundings to bfloat16 on the way count: a program that leaves them out, or rounds other values in their place, can miss the bound.
Values may be sent and summed in bfloat16 or wider, within the bound.
A program may use at most 128 MiB of HBM per device.

v0:
```python
import jax
import jax.numpy as jnp
from jax import lax
from jax.sharding import PartitionSpec as P


def with_halo(shard, sides, width):
    for axis, dim in sides:
        count, length = (lax.axis_size(axis), shard.shape[dim])
        up = [(i, (i + 1) % count) for i in range(count - 1)]
        down = [(j, i) for i, j in up]
        last = lax.slice_in_dim(shard, length - width, length, axis=dim)
        leading = lax.slice_in_dim(shard, 0, width, axis=dim)
        before = lax.ppermute(last, axis, up)
        after = lax.ppermute(leading, axis, down)
        shard = jnp.concatenate([before, shard, after], axis=dim)
    return shard


def leaky(value):
    return jnp.where(value > 0, value, 0.3 * value)


def slope(value):
    return jnp.where(value > 0, 1.0, 0.3)


def pooled(value):
    shape = value.shape
    blocks = value.reshape(shape[0], shape[1], shape[2] // 2, 2, shape[3] // 2, 2, shape[4] // 2, 2)
    return blocks.mean(axis=(3, 5, 7))


def widened(value):
    shape = value.shape
    spread = jnp.broadcast_to(
        value[:, :, :, None, :, None, :, None],
        (shape[0], shape[1], shape[2], 2, shape[3], 2, shape[4], 2),
    )
    return spread.reshape(shape[0], shape[1], 2 * shape[2], 2 * shape[3], 2 * shape[4])


def convolve(source, kernel):
    return lax.conv_general_dilated(
        source,
        kernel,
        (1, 1, 1),
        ((0, 0), (1, 1), (1, 1)),
        dimension_numbers=("NCDHW", "DHWIO", "NCDHW"),
        preferred_element_type=jnp.float32,
    )


def flipped(kernel):
    return jnp.transpose(kernel[::-1, ::-1, ::-1], (0, 1, 2, 4, 3))


def filter_grad(source, gradient):
    planes, extent_y, extent_z = (gradient.shape[2], gradient.shape[3], gradient.shape[4])
    padded = jnp.pad(source, ((0, 0), (0, 0), (0, 0), (1, 1), (1, 1)))
    partials = []
    for offset in range(27):
        shift_a, shift_b, shift_c = (offset // 9, offset // 3 % 3, offset % 3)
        window = padded[
            :,
            :,
            shift_a : shift_a + planes,
            shift_b : shift_b + extent_y,
            shift_c : shift_c + extent_z,
        ]
        partials.append(
            jnp.einsum("bcxyz,bdxyz->cd", window, gradient, preferred_element_type=jnp.float32)
        )
    return jnp.stack(partials).reshape(3, 3, 3, source.shape[1], gradient.shape[1])


def local(crop, filter_one, filter_two, cotangent):
    crop_wide = with_halo(crop, (("space", 2),), 1)
    z_one = convolve(crop_wide, filter_one)
    maps_one = pooled(leaky(z_one)).astype(jnp.bfloat16)
    maps_wide = with_halo(maps_one, (("space", 2),), 1)
    z_two = convolve(maps_wide, filter_two)
    grad_pre_two = (slope(z_two) * widened(cotangent.astype(jnp.float32)) * 0.125).astype(
        jnp.bfloat16
    )
    grad_outer = with_halo(grad_pre_two, (("space", 2),), 1)
    features = pooled(leaky(z_two)).astype(jnp.bfloat16)
    local_two = filter_grad(maps_wide, grad_pre_two)
    back_one = convolve(grad_outer, flipped(filter_two))
    grad_pre_one = (slope(z_one) * widened(back_one) * 0.125).astype(jnp.bfloat16)
    local_one = filter_grad(crop_wide, grad_pre_one)
    grad_one, grad_two = lax.psum((local_one, local_two), ("dp", "space"))
    return (features, grad_one, grad_two)


def solution(mesh):
    placed = (P("dp", None, "space", None, None), P(), P(), P("dp", None, "space", None, None))
    return jax.shard_map(
        local,
        mesh=mesh,
        in_specs=placed,
        out_specs=(P("dp", None, "space", None, None), P(), P()),
        check_vma=False,
    )
```

profile of v0, /device:TPU:1, one launch (start us, length us, event | category | flops | bytes accessed | tf_op | source)
XLA Modules:
  0.0 399.3 jit_solution(16076839817375526808)
XLA Ops:
  7.2 1.2 copy.322
  8.5 4.6 %collective-permute-start = (bf16[1,4,1,64,64]{4,1,3,2,0:T(4,128)(2,1)S(1)}, bf16[1,4,1,64,64]{4,1,3,2,0:T(4,128)(2,1)S(1)}, u32[]{:S(2)}, u32[]{:S(2)}) collective-permute-start(bf16[1,4,1,64,64]{4,1,3,2,0:T(4,128)(2,1)S(1)} %get-tuple-element.20), channel_id=1, source_target_pairs={{0,1},{1,2},{2,3},{3,4},{4,5},{5,6},{6,7},{7,8},{8,9},{9,10},{10,1... | collective-permute-start | bytes 98312 | tf_op jit(solution)/shard_map/ppermute | solution.py:14
  13.1 1.9 collective-permute-start.1
  15.7 1.2 constant_dynamic-update-slice_fusion.1
  16.9 1.8 collective-permute-done.1
  19.8 3.7 copy.327
  23.6 1.7 slice.254
  25.2 24.3 %compare_select_fusion = (f32[4,64,8,9,32]{4,2,3,1,0:T(8,128)}, f32[4,64,8,9,32]{4,2,3,1,0:T(8,128)}) fusion(pred[8,9]{0,1:T(8,128)(4,1)S(1)} %copy-done.15, bf16[3,3,3,4,32]{4,3,2,1,0:T(4,128)(2,1)S(1)} %copy-done.14, bf16[4,6,64,1,7,2]{4,0,5,2,1,3:T(4,128)(2,1)S(1)} %slice.254, bf16[4,6,64,1,8,9]{4,0,5,2,1,3:T(4,128)(2,1)} %copy.327), kind=kOutput, calls=%fused_computation.1 | convolution fusion | flops 129835008 | bytes 4989768 | tf_op jit(solution)/shard_map/conv_general_dilated | solution.py:44
  49.5 8.7 %copy.328 = f32[4,64,8,9,32]{1,4,3,2,0:T(8,128)} copy(f32[4,64,8,9,32]{4,2,3,1,0:T(8,128)} %get-tuple-element.10) | data formatting | bytes 4718592 | tf_op jit(solution)/shard_map/jit(_where)/select_n | solution.py:21
  58.2 4.6 %slice_bitcast_fusion.1 = f32[1,32,4,64,64]{3,1,4,2,0:T(8,128)} fusion(f32[4,64,1,72,32]{1,4,3,0,2:T(8,128)} %bitcast.701), kind=kLoop, calls=%fused_computation.14 | loop fusion | bytes 4194304 | tf_op jit(solution)/shard_map/jit(_where)/select_n | solution.py:21
  62.8 9.3 %copy.329 = f32[1,32,4,64,64]{1,4,3,2,0:T(8,128)} copy(f32[1,32,4,64,64]{3,1,4,2,0:T(8,128)} %slice_bitcast_fusion.1) | data formatting | bytes 4194304 | tf_op jit(solution)/shard_map/jit(_where)/select_n | solution.py:21
  72.1 9.1 %reduce_sum.21 = f32[32,2,32,32]{0,3,2,1:T(8,128)S(1)} reduce(f32[32,2,2,32,2,32,2]{0,6,5,4,3,2,1:T(2,128)} %bitcast.698, f32[]{:T(128)} %constant.5.clone.1), dimensions={2,4,6}, to_apply=%region_0.1 | reduce | flops 458752 | bytes 2359300 | tf_op jit(solution)/shard_map/reduce_sum | solution.py:31
  81.7 0.7 fusion.295
  82.5 1.9 collective-permute-start.2
  84.4 2.4 collective-permute-start.3
  87.5 0.9 copy.357
  88.4 8.7 %copy.335 = f32[4,64,8,9,32]{1,4,3,2,0:T(8,128)} copy(f32[4,64,8,9,32]{4,2,3,1,0:T(8,128)} %get-tuple-element.9) | data formatting | bytes 4718592 | tf_op jit(solution)/shard_map/jit(_where)/select_n | solution.py:25
  97.8 2.3 pad_maximum_fusion
  100.1 3.8 copy.455
  103.9 2.6 pad.12.clone
  106.5 3.0 copy.333
  109.5 1.2 slice.258
  110.7 4.6 %compare_select_fusion.1 = (f32[2,32,8,5,64]{4,2,3,1,0:T(8,128)S(1)}, f32[2,32,8,5,64]{4,2,3,1,0:T(8,128)}) fusion(bf16[3,3,3,32,64]{4,3,2,1,0:T(8,128)(2,1)S(1)} %copy-done, bf16[32,4,32,1,7,2]{0,4,5,2,1,3:T(8,128)(2,1)S(1)} %slice.258, bf16[32,4,32,1,8,5]{0,4,5,2,1,3:T(8,128)(2,1)} %copy.333, pred[8,5]{0,1:T(8,128)(4,1)S(1)} %copy-done.16), kind=kOutput, calls=%fused_computation.34 | convolution fusion | flops 279412736 | bytes 1863720 | tf_op jit(solution)/shard_map/conv_general_dilated | solution.py:44
  116.7 1.0 fusion.91
  131.9 1.5 fusion.39
  136.0 0.8 copy-done.5
  136.9 3.1 collective-permute-start.4
  140.0 2.1 collective-permute-start.5
  142.1 1.6 copy.334
  144.9 2.8 collective-permute-done.5
  148.9 5.1 %fusion.32 = f32[2,32,8,5,32]{4,2,3,1,0:T(8,128)S(1)} fusion(bf16[3,3,3,32,64]{4,3,2,1,0:T(8,128)(2,1)S(1)} %copy-done, bf16[64,4,32,1,7,2]{0,4,5,2,1,3:T(8,128)(2,1)S(1)} %slice.264, bf16[64,4,32,1,8,5]{0,4,5,2,1,3:T(8,128)(2,1)S(1)} %copy.339, pred[8,5]{0,1:T(8,128)(4,1)S(1)} %copy-done.16), kind=kOutput, calls=%fused_computation.36 | convolution fusion | flops 280051712 | bytes 1323048 | tf_op jit(solution)/shard_map/conv_general_dilated | solution.py:44
  155.0 7.6 %broadcast_in_dim.44 = f32[32,2,2,32,2,32,2]{0,6,5,4,3,2,1:T(2,128)} broadcast(f32[32,2,32,32]{0,3,2,1:T(8,128)S(1)} %copy.341), dimensions={0,1,3,5} | broadcast | bytes 2359296 | tf_op jit(solution)/shard_map/broadcast_in_dim | solution.py:36
  162.6 7.8 %copy.342 = f32[1,32,4,64,64]{3,1,4,2,0:T(8,128)} copy(f32[1,32,4,64,64]{1,4,3,2,0:T(8,128)} %bitcast.699) | data formatting | bytes 4194304 | tf_op jit(solution)/shard_map/broadcast_in_dim | solution.py:36
  170.4 5.8 %fusion.14 = bf16[32,4,64,64]{2,0,3,1:T(8,128)(2,1)} fusion(f32[1,32,4,64,64]{3,1,4,2,0:T(8,128)} %copy.342, f32[4,64,1,72,32]{1,4,3,0,2:T(8,128)} %bitcast.700), kind=kLoop, calls=%fused_computation.20 | loop fusion | flops 1572864 | bytes 5242880 | tf_op jit(solution)/shard_map/reshape.3
  176.3 5.7 %copy.343 = bf16[32,4,64,64]{3,0,2,1:T(8,128)(2,1)S(1)} copy(bf16[32,4,64,64]{2,0,3,1:T(8,128)(2,1)} %fusion.14) | data formatting | bytes 2097152 | tf_op jit(solution)/shard_map/reshape.3
  184.0 0.7 fusion.85
  185.4 0.7 fusion.83
  186.1 0.7 fusion.82
  188.3 0.7 fusion.79
  190.4 0.7 fusion.76
  191.9 0.7 fusion.74
  192.6 0.7 fusion.73
  196.9 0.7 fusion.67
  198.3 0.7 fusion.65
  199.0 0.7 fusion.64
  201.1 85.7 %psum.14 = f32[3,3,3,4,32]{4,3,2,1,0:T(4,128)} all-reduce(f32[3,3,3,4,32]{4,3,2,1,0:T(4,128)S(1)} %bitcast.714), channel_id=1, replica_groups=mesh['dp'=8,'space'=32] {'dp','space'}, use_global_device_ids=true, to_apply=%region_3.4 | all-reduce | flops 3456 | bytes 27648 | tf_op jit(solution)/shard_map/psum | solution.py:92
  286.8 103.6 %all-reduce.4.cloned.1.call-done = f32[3,3,3,32,64]{4,3,2,1,0:T(8,128)} async-done(((f32[3,3,3,32,64]{4,3,2,1,0:T(8,128)}), f32[3,3,3,32,64]{4,3,2,1,0:T(8,128)}) %all-reduce.4.cloned.1.call-update) | async-done | bytes 221200 | tf_op jit(solution)/shard_map/psum | solution.py:92
  390.4 1.8 copy.566
  (106 shorter events, 36.9 us)
Async XLA Ops:
  7.2 103.6 %copy-start = (bf16[3,3,3,32,64]{4,3,2,1,0:T(8,128)(2,1)S(1)}, bf16[3,3,3,32,64]{4,3,2,1,0:T(8,128)(2,1)}, u32[]{:S(2)}) copy-start(bf16[3,3,3,32,64]{4,3,2,1,0:T(8,128)(2,1)} %param.6) | copy-start | bytes 331780
  7.2 383.2 %all-reduce.4.cloned.1.call-start = ((), (), s32[]{:S(2)}) async-start(), calls=%async_computation | async-start | bytes 884736 | tf_op jit(solution)/shard_map/psum | solution.py:92
  8.5 6.5 %collective-permute-start = (bf16[1,4,1,64,64]{4,1,3,2,0:T(4,128)(2,1)S(1)}, bf16[1,4,1,64,64]{4,1,3,2,0:T(4,128)(2,1)S(1)}, u32[]{:S(2)}, u32[]{:S(2)}) collective-permute-start(bf16[1,4,1,64,64]{4,1,3,2,0:T(4,128)(2,1)S(1)} %get-tuple-element.20), channel_id=1, source_target_pairs={{0,1},{1,2},{2,3},{3,4},{4,5},{5,6},{6,7},{7,8},{8,9},{9,10},{10,1... | collective-permute-start | bytes 98312 | tf_op jit(solution)/shard_map/ppermute | solution.py:14
  13.1 5.6 %collective-permute-start.1 = (bf16[1,4,1,64,64]{4,1,3,2,0:T(4,128)(2,1)S(1)}, bf16[1,4,1,64,64]{4,1,3,2,0:T(4,128)(2,1)S(1)}, u32[]{:S(2)}, u32[]{:S(2)}) collective-permute-start(bf16[1,4,1,64,64]{4,1,3,2,0:T(4,128)(2,1)S(1)} %get-tuple-element.19), channel_id=1, source_target_pairs={{1,0},{2,1},{3,2},{4,3},{5,4},{6,5},{7,6},{8,7},{9,8},{10,9},{11,1... | collective-permute-start | bytes 98312 | tf_op jit(solution)/shard_map/ppermute | solution.py:15
  15.0 0.6 copy-start.10
  18.7 0.6 copy-start.8
  19.8 5.4 %copy-start.14 = (bf16[3,3,3,4,32]{4,3,2,1,0:T(4,128)(2,1)S(1)}, bf16[3,3,3,4,32]{4,3,2,1,0:T(4,128)(2,1)}, u32[]{:S(2)}) copy-start(bf16[3,3,3,4,32]{4,3,2,1,0:T(4,128)(2,1)} %param.5) | copy-start | bytes 20740
  19.8 5.4 %copy-start.15 = (pred[8,9]{0,1:T(8,128)(4,1)S(1)}, pred[8,9]{0,1:T(8,128)(4,1)}, u32[]{:S(2)}) copy-start(pred[8,9]{0,1:T(8,128)(4,1)} %constant.39) | copy-start | bytes 220
  81.6 5.2 %copy-start.13 = (bf16[1,64,1,16,16]{1,4,3,2,0:T(8,128)(2,1)S(1)}, bf16[1,64,1,16,16]{1,4,3,2,0:T(8,128)(2,1)}, u32[]{:S(2)}) copy-start(bf16[1,64,1,16,16]{1,4,3,2,0:T(8,128)(2,1)} %param.7) | copy-start | bytes 98308
  81.6 5.9 %copy-start.3 = (bf16[1,4,4,64,64]{4,3,2,1,0:T(8,128)(2,1)S(1)}, bf16[1,4,4,64,64]{4,3,2,1,0:T(8,128)(2,1)}, u32[]{:S(2)}) copy-start(bf16[1,4,4,64,64]{4,3,2,1,0:T(8,128)(2,1)} %param.4) | copy-start | bytes 393220
  82.5 14.6 %collective-permute-start.2 = (bf16[1,32,1,32,32]{4,1,3,2,0:T(8,128)(2,1)}, bf16[1,32,1,32,32]{4,1,3,2,0:T(8,128)(2,1)S(1)}, u32[]{:S(2)}, u32[]{:S(2)}) collective-permute-start(bf16[1,32,1,32,32]{4,1,3,2,0:T(8,128)(2,1)} %get-tuple-element.17), channel_id=1, source_target_pairs={{0,1},{1,2},{2,3},{3,4},{4,5},{5,6},{6,7},{7,8},{8,9},{9,10},{10,1... | collective-permute-start | bytes 196616 | tf_op jit(solution)/shard_map/ppermute | solution.py:14
  84.4 13.4 %collective-permute-start.3 = (bf16[1,32,1,32,32]{4,1,3,2,0:T(8,128)(2,1)S(1)}, bf16[1,32,1,32,32]{4,1,3,2,0:T(8,128)(2,1)}, u32[]{:S(2)}, u32[]{:S(2)}) collective-permute-start(bf16[1,32,1,32,32]{4,1,3,2,0:T(8,128)(2,1)S(1)} %get-tuple-element.18), channel_id=1, source_target_pairs={{1,0},{2,1},{3,2},{4,3},{5,4},{6,5},{7,6},{8,7},{9,8},{10,9},{11,1... | collective-permute-start | bytes 196616 | tf_op jit(solution)/shard_map/ppermute | solution.py:15
  97.1 0.7 copy-start.6
  106.5 4.2 %copy-start.16 = (pred[8,5]{0,1:T(8,128)(4,1)S(1)}, pred[8,5]{0,1:T(8,128)(4,1)}, u32[]{:S(2)}) copy-start(pred[8,5]{0,1:T(8,128)(4,1)} %constant.38) | copy-start | bytes 124
  115.4 0.9 copy-start.4
  118.3 1.9 copy-start.7
  134.8 2.0 copy-start.2
  136.0 0.8 copy-start.5
  136.9 8.1 %collective-permute-start.4 = (bf16[1,64,1,32,32]{1,3,4,2,0:T(8,128)(2,1)S(1)}, bf16[1,64,1,32,32]{1,3,4,2,0:T(8,128)(2,1)S(1)}, u32[]{:S(2)}, u32[]{:S(2)}) collective-permute-start(bf16[1,64,1,32,32]{1,3,4,2,0:T(8,128)(2,1)S(1)} %get-tuple-element.15), channel_id=1, source_target_pairs={{0,1},{1,2},{2,3},{3,4},{4,5},{5,6},{6,7},{7,8},{8,9},{9,10},{10,1... | collective-permute-start | bytes 393224 | tf_op jit(solution)/shard_map/ppermute | solution.py:14
  140.0 7.7 %collective-permute-start.5 = (bf16[1,64,1,32,32]{1,3,4,2,0:T(8,128)(2,1)S(1)}, bf16[1,64,1,32,32]{1,3,4,2,0:T(8,128)(2,1)S(1)}, u32[]{:S(2)}, u32[]{:S(2)}) collective-permute-start(bf16[1,64,1,32,32]{1,3,4,2,0:T(8,128)(2,1)S(1)} %get-tuple-element.16), channel_id=1, source_target_pairs={{1,0},{2,1},{3,2},{4,3},{5,4},{6,5},{7,6},{8,7},{9,8},{10,9},{11,1... | collective-permute-start | bytes 393224 | tf_op jit(solution)/shard_map/ppermute | solution.py:15
  183.3 1.5 copy-start.11
  189.6 1.6 copy-start.1
  189.6 1.6 copy-start.12
  196.1 1.5 copy-start.9
Sparse Core Ops, SparseCore 0:
  136.9 253.4 all-reduce.3
where the time goes:
time: 407 us; the launch traced here: 399 us
  waiting for transfers between devices  108 us (27%)
  blocking collectives  85.7 us (21%)
  local copies, waits for them, and re-layouts  83.9 us (21%)
  matrix products  71.1 us (17%)
  other arithmetic  19.3 us (5%)
  starting transfers between devices  16.1 us (4%)
  between operations  14.9 us (4%)
    psum x1, waiting for transfers between devices, local(): grad_one, grad_two = lax.psum((local_one, local_two), ('dp', 'space'))  104 us
    psum x1, blocking collectives, local(): grad_one, grad_two = lax.psum((local_one, local_two), ('dp', 'space'))  85.7 us
    dot_general x54, matrix products, filter_grad(): jnp.einsum('bcxyz,bdxyz->cd', window, gradient, preferred_element_type=jn...  37.1 us
    conv_general_dilated x3, matrix products, convolve(): lax.conv_general_dilated(source, kernel, (1, 1, 1), ((0, 0), (1, 1), (1,...  34 us
    select_n x4, local copies, waits for them, and re-layouts, leaky(): return jnp.where(value > 0, value, 0.3 * value)  24.2 us
    broadcast_in_dim x6, local copies, waits for them, and re-layouts, widened(): jnp.broadcast_to(value[:, :, :, None, :, None, :, None], (shape[0], shape...  17.1 us
    unnamed x41, local copies, waits for them, and re-layouts  12.5 us
    conv_general_dilated x7, local copies, waits for them, and re-layouts, convolve(): lax.conv_general_dilated(source, kernel, (1, 1, 1), ((0, 0), (1, 1), (1,...  10.5 us
  transfers between devices with their start and end apart: 7, of which 3 were waited for; matrix products, arithmetic and copies ran while one was open for 17% of the time, Pallas kernels for 0%

commit v1 on v0

--- a/solution.py
+++ b/solution.py
@@ -89,7 +89,7 @@
     back_one = convolve(grad_outer, flipped(filter_two))
     grad_pre_one = (slope(z_one) * widened(back_one) * 0.125).astype(jnp.bfloat16)
     local_one = filter_grad(crop_wide, grad_pre_one)
-    grad_one, grad_two = lax.psum((local_one, local_two), ("dp", "space"))
+    grad_one, grad_two = lax.psum(lax.psum((local_one, local_two), "dp"), "space")
     return (features, grad_one, grad_two)
 
 

time: 407 us -> 532 us (1.31)
  blocking collectives: 85.7 us -> 181 us
  waiting for transfers between devices: 108 us -> 138 us
    psum x1 -> x2, blocking collectives: 85.7 us -> 181 us  [the longest x1 139 us: local(): lax.psum(lax.psum((local_one, local_two), 'dp'), 'space')]
    psum x1 -> x2, waiting for transfers between devices: 104 us -> 133 us  [the longest x1 90.1 us: local(): lax.psum(lax.psum((local_one, local_two), 'dp'), 'space')]
  transfers between devices with their start and end apart: 7 -> 8, of which waited for: 3 -> 4; matrix products, arithmetic and copies ran while one was open for 17% -> 13% of each run, Pallas kernels for 0% -> 0%
where the time goes in v1:
time: 532 us; the launch traced here: 524 us
  blocking collectives  181 us (34%)
  waiting for transfers between devices  138 us (26%)
  local copies, waits for them, and re-layouts  83.9 us (16%)
  matrix products  71.1 us (13%)
  other arithmetic  19.3 us (4%)
  starting transfers between devices  16.2 us (3%)
  between operations  14.9 us (3%)
    psum x1, blocking collectives, local(): lax.psum(lax.psum((local_one, local_two), 'dp'), 'space')  139 us
    psum x1, waiting for transfers between devices, local(): lax.psum(lax.psum((local_one, local_two), 'dp'), 'space')  90.1 us
    psum x1, waiting for transfers between devices, local(): lax.psum((local_one, local_two), 'dp')  43 us
    psum x1, blocking collectives, local(): lax.psum((local_one, local_two), 'dp')  41.8 us
    dot_general x54, matrix products, filter_grad(): jnp.einsum('bcxyz,bdxyz->cd', window, gradient, preferred_element_type=jn...  37.1 us
    conv_general_dilated x3, matrix products, convolve(): lax.conv_general_dilated(source, kernel, (1, 1, 1), ((0, 0), (1, 1), (1,...  34 us
    select_n x4, local copies, waits for them, and re-layouts, leaky(): return jnp.where(value > 0, value, 0.3 * value)  24.2 us
    broadcast_in_dim x6, local copies, waits for them, and re-layouts, widened(): jnp.broadcast_to(value[:, :, :, None, :, None, :, None], (shape[0], shape...  17.1 us
  transfers between devices with their start and end apart: 8, of which 4 were waited for; matrix products, arithmetic and copies ran while one was open for 13% of the time, Pallas kernels for 0%

profile of v1, /device:TPU:1, one launch (start us, length us, event | category | flops | bytes accessed | tf_op | source)
XLA Modules:
  0.0 524.3 jit_solution(18237478992681271443)
XLA Ops:
  7.2 1.2 copy.322
  8.5 4.6 collective-permute-start
  13.1 1.9 collective-permute-start.1
  15.7 1.2 constant_dynamic-update-slice_fusion.1
  16.9 1.8 collective-permute-done.1
  19.8 3.7 copy.327
  23.5 1.7 slice.254
  25.2 24.2 %compare_select_fusion = (f32[4,64,8,9,32]{4,2,3,1,0:T(8,128)}, f32[4,64,8,9,32]{4,2,3,1,0:T(8,128)}) fusion(pred[8,9]{0,1:T(8,128)(4,1)S(1)} %copy-done.15, bf16[3,3,3,4,32]{4,3,2,1,0:T(4,128)(2,1)S(1)} %copy-done.14, bf16[4,6,64,1,7,2]{4,0,5,2,1,3:T(4,128)(2,1)S(1)} %slice.254, bf16[4,6,64,1,8,9]{4,0,5,2,1,3:T(4,128)(2,1)} %copy.327), kind=kOutput, calls=%fused_computation.1 | convolution fusion | flops 129835008 | bytes 4989768 | tf_op jit(solution)/shard_map/conv_general_dilated | solution.py:44
  49.5 8.7 %copy.328 = f32[4,64,8,9,32]{1,4,3,2,0:T(8,128)} copy(f32[4,64,8,9,32]{4,2,3,1,0:T(8,128)} %get-tuple-element.10) | data formatting | bytes 4718592 | tf_op jit(solution)/shard_map/jit(_where)/select_n | solution.py:21
  58.1 4.6 slice_bitcast_fusion.1
  62.7 9.3 %copy.329 = f32[1,32,4,64,64]{1,4,3,2,0:T(8,128)} copy(f32[1,32,4,64,64]{3,1,4,2,0:T(8,128)} %slice_bitcast_fusion.1) | data formatting | bytes 4194304 | tf_op jit(solution)/shard_map/jit(_where)/select_n | solution.py:21
  72.1 9.1 %reduce_sum.21 = f32[32,2,32,32]{0,3,2,1:T(8,128)S(1)} reduce(f32[32,2,2,32,2,32,2]{0,6,5,4,3,2,1:T(2,128)} %bitcast.698, f32[]{:T(128)} %constant.5.clone.1), dimensions={2,4,6}, to_apply=%region_0.1 | reduce | flops 458752 | bytes 2359300 | tf_op jit(solution)/shard_map/reduce_sum | solution.py:31
  81.7 0.7 fusion.295
  82.4 1.9 collective-permute-start.2
  84.3 2.4 collective-permute-start.3
  87.5 0.9 copy.357
  88.3 8.7 %copy.335 = f32[4,64,8,9,32]{1,4,3,2,0:T(8,128)} copy(f32[4,64,8,9,32]{4,2,3,1,0:T(8,128)} %get-tuple-element.9) | data formatting | bytes 4718592 | tf_op jit(solution)/shard_map/jit(_where)/select_n | solution.py:25
  97.7 2.3 pad_maximum_fusion
  100.0 3.8 copy.455
  103.9 2.6 pad.12.clone
  106.4 3.0 copy.333
  109.4 1.2 slice.258
  110.6 4.6 compare_select_fusion.1
  116.6 1.0 fusion.91
  131.7 1.5 fusion.39
  135.9 0.8 copy-done.5
  136.8 3.1 collective-permute-start.4
  139.9 2.1 collective-permute-start.5
  142.0 1.6 copy.334
  144.9 2.8 collective-permute-done.5
  148.8 5.1 fusion.32
  154.9 7.6 %broadcast_in_dim.44 = f32[32,2,2,32,2,32,2]{0,6,5,4,3,2,1:T(2,128)} broadcast(f32[32,2,32,32]{0,3,2,1:T(8,128)S(1)} %copy.341), dimensions={0,1,3,5} | broadcast | bytes 2359296 | tf_op jit(solution)/shard_map/broadcast_in_dim | solution.py:36
  162.5 7.8 %copy.342 = f32[1,32,4,64,64]{3,1,4,2,0:T(8,128)} copy(f32[1,32,4,64,64]{1,4,3,2,0:T(8,128)} %bitcast.699) | data formatting | bytes 4194304 | tf_op jit(solution)/shard_map/broadcast_in_dim | solution.py:36
  170.3 5.8 %fusion.14 = bf16[32,4,64,64]{2,0,3,1:T(8,128)(2,1)} fusion(f32[1,32,4,64,64]{3,1,4,2,0:T(8,128)} %copy.342, f32[4,64,1,72,32]{1,4,3,0,2:T(8,128)} %bitcast.700), kind=kLoop, calls=%fused_computation.20 | loop fusion | flops 1572864 | bytes 5242880 | tf_op jit(solution)/shard_map/reshape.3
  176.2 5.7 %copy.343 = bf16[32,4,64,64]{3,0,2,1:T(8,128)(2,1)S(1)} copy(bf16[32,4,64,64]{2,0,3,1:T(8,128)(2,1)} %fusion.14) | data formatting | bytes 2097152 | tf_op jit(solution)/shard_map/reshape.3
  184.0 0.7 fusion.85
  185.3 0.7 fusion.83
  186.1 0.7 fusion.82
  190.3 0.7 fusion.76
  191.9 0.7 fusion.74
  192.6 0.7 fusion.73
  196.8 0.7 fusion.67
  198.2 0.7 fusion.65
  200.3 43.0 %all-reduce.5.cloned.1.call-done = f32[3,3,3,32,64]{4,3,2,1,0:T(8,128)} async-done(((f32[3,3,3,32,64]{4,3,2,1,0:T(8,128)}), f32[3,3,3,32,64]{4,3,2,1,0:T(8,128)}) %all-reduce.5.cloned.1.call-update) | async-done | bytes 221200 | tf_op jit(solution)/shard_map/psum | solution.py:92
  244.1 41.8 %psum.28 = f32[3,3,3,4,32]{4,3,2,1,0:T(4,128)S(1)} all-reduce(f32[3,3,3,4,32]{4,3,2,1,0:T(4,128)S(1)} %bitcast.714), channel_id=1, replica_groups=mesh['dp'=8,'space'=32] {'dp'}, use_global_device_ids=true, to_apply=%region_3.4 | all-reduce | flops 3456 | bytes 27648 | tf_op jit(solution)/shard_map/psum | solution.py:92
  285.9 139.4 %psum.29 = f32[3,3,3,4,32]{4,3,2,1,0:T(4,128)} all-reduce(f32[3,3,3,4,32]{4,3,2,1,0:T(4,128)S(1)} %psum.28), channel_id=1, replica_groups=mesh['dp'=8,'space'=32] {'space'}, use_global_device_ids=true, to_apply=%region_4.5 | all-reduce | flops 3456 | bytes 27648 | tf_op jit(solution)/shard_map/psum | solution.py:92
  425.3 90.1 %all-reduce.7.cloned.1.call-done = f32[3,3,3,32,64]{4,3,2,1,0:T(8,128)} async-done(((f32[3,3,3,32,64]{4,3,2,1,0:T(8,128)}), f32[3,3,3,32,64]{4,3,2,1,0:T(8,128)}) %all-reduce.7.cloned.1.call-update) | async-done | bytes 221200 | tf_op jit(solution)/shard_map/psum | solution.py:92
  515.4 1.8 copy.567
  (110 shorter events, 38.4 us)
Async XLA Ops:
  7.2 103.5 %copy-start = (bf16[3,3,3,32,64]{4,3,2,1,0:T(8,128)(2,1)S(1)}, bf16[3,3,3,32,64]{4,3,2,1,0:T(8,128)(2,1)}, u32[]{:S(2)}) copy-start(bf16[3,3,3,32,64]{4,3,2,1,0:T(8,128)(2,1)} %param.6) | copy-start | bytes 331780
  7.2 236.2 %all-reduce.5.cloned.1.call-start = ((), (), s32[]{:S(2)}) async-start(), calls=%async_computation | async-start | bytes 884736 | tf_op jit(solution)/shard_map/psum | solution.py:92
  8.5 6.5 %collective-permute-start = (bf16[1,4,1,64,64]{4,1,3,2,0:T(4,128)(2,1)S(1)}, bf16[1,4,1,64,64]{4,1,3,2,0:T(4,128)(2,1)S(1)}, u32[]{:S(2)}, u32[]{:S(2)}) collective-permute-start(bf16[1,4,1,64,64]{4,1,3,2,0:T(4,128)(2,1)S(1)} %get-tuple-element.20), channel_id=1, source_target_pairs={{0,1},{1,2},{2,3},{3,4},{4,5},{5,6},{6,7},{7,8},{8,9},{9,10},{10,1... | collective-permute-start | bytes 98312 | tf_op jit(solution)/shard_map/ppermute | solution.py:14
  13.1 5.6 %collective-permute-start.1 = (bf16[1,4,1,64,64]{4,1,3,2,0:T(4,128)(2,1)S(1)}, bf16[1,4,1,64,64]{4,1,3,2,0:T(4,128)(2,1)S(1)}, u32[]{:S(2)}, u32[]{:S(2)}) collective-permute-start(bf16[1,4,1,64,64]{4,1,3,2,0:T(4,128)(2,1)S(1)} %get-tuple-element.19), channel_id=1, source_target_pairs={{1,0},{2,1},{3,2},{4,3},{5,4},{6,5},{7,6},{8,7},{9,8},{10,9},{11,1... | collective-permute-start | bytes 98312 | tf_op jit(solution)/shard_map/ppermute | solution.py:15
  15.0 0.6 copy-start.10
  18.7 0.6 copy-start.8
  19.8 5.4 %copy-start.14 = (bf16[3,3,3,4,32]{4,3,2,1,0:T(4,128)(2,1)S(1)}, bf16[3,3,3,4,32]{4,3,2,1,0:T(4,128)(2,1)}, u32[]{:S(2)}) copy-start(bf16[3,3,3,4,32]{4,3,2,1,0:T(4,128)(2,1)} %param.5) | copy-start | bytes 20740
  19.8 5.4 %copy-start.15 = (pred[8,9]{0,1:T(8,128)(4,1)S(1)}, pred[8,9]{0,1:T(8,128)(4,1)}, u32[]{:S(2)}) copy-start(pred[8,9]{0,1:T(8,128)(4,1)} %constant.39) | copy-start | bytes 220
  81.5 5.2 copy-start.13
  81.5 5.9 %copy-start.3 = (bf16[1,4,4,64,64]{4,3,2,1,0:T(8,128)(2,1)S(1)}, bf16[1,4,4,64,64]{4,3,2,1,0:T(8,128)(2,1)}, u32[]{:S(2)}) copy-start(bf16[1,4,4,64,64]{4,3,2,1,0:T(8,128)(2,1)} %param.4) | copy-start | bytes 393220
  82.4 14.6 %collective-permute-start.2 = (bf16[1,32,1,32,32]{4,1,3,2,0:T(8,128)(2,1)}, bf16[1,32,1,32,32]{4,1,3,2,0:T(8,128)(2,1)S(1)}, u32[]{:S(2)}, u32[]{:S(2)}) collective-permute-start(bf16[1,32,1,32,32]{4,1,3,2,0:T(8,128)(2,1)} %get-tuple-element.17), channel_id=1, source_target_pairs={{0,1},{1,2},{2,3},{3,4},{4,5},{5,6},{6,7},{7,8},{8,9},{9,10},{10,1... | collective-permute-start | bytes 196616 | tf_op jit(solution)/shard_map/ppermute | solution.py:14
  84.3 13.4 %collective-permute-start.3 = (bf16[1,32,1,32,32]{4,1,3,2,0:T(8,128)(2,1)S(1)}, bf16[1,32,1,32,32]{4,1,3,2,0:T(8,128)(2,1)}, u32[]{:S(2)}, u32[]{:S(2)}) collective-permute-start(bf16[1,32,1,32,32]{4,1,3,2,0:T(8,128)(2,1)S(1)} %get-tuple-element.18), channel_id=1, source_target_pairs={{1,0},{2,1},{3,2},{4,3},{5,4},{6,5},{7,6},{8,7},{9,8},{10,9},{11,1... | collective-permute-start | bytes 196616 | tf_op jit(solution)/shard_map/ppermute | solution.py:15
  97.0 0.7 copy-start.6
  106.4 4.2 copy-start.16
  115.3 0.9 copy-start.4
  118.2 1.9 copy-start.7
  134.6 2.1 copy-start.2
  135.9 0.8 copy-start.5
  136.7 378.7 %all-reduce.7.cloned.1.call-start = ((), (), s32[]{:S(2)}) async-start(), calls=%async_computation.1 | async-start | bytes 884736 | tf_op jit(solution)/shard_map/psum | solution.py:92
  136.8 8.1 %collective-permute-start.4 = (bf16[1,64,1,32,32]{1,3,4,2,0:T(8,128)(2,1)S(1)}, bf16[1,64,1,32,32]{1,3,4,2,0:T(8,128)(2,1)S(1)}, u32[]{:S(2)}, u32[]{:S(2)}) collective-permute-start(bf16[1,64,1,32,32]{1,3,4,2,0:T(8,128)(2,1)S(1)} %get-tuple-element.15), channel_id=1, source_target_pairs={{0,1},{1,2},{2,3},{3,4},{4,5},{5,6},{6,7},{7,8},{8,9},{9,10},{10,1... | collective-permute-start | bytes 393224 | tf_op jit(solution)/shard_map/ppermute | solution.py:14
  139.9 7.7 %collective-permute-start.5 = (bf16[1,64,1,32,32]{1,3,4,2,0:T(8,128)(2,1)S(1)}, bf16[1,64,1,32,32]{1,3,4,2,0:T(8,128)(2,1)S(1)}, u32[]{:S(2)}, u32[]{:S(2)}) collective-permute-start(bf16[1,64,1,32,32]{1,3,4,2,0:T(8,128)(2,1)S(1)} %get-tuple-element.16), channel_id=1, source_target_pairs={{1,0},{2,1},{3,2},{4,3},{5,4},{6,5},{7,6},{8,7},{9,8},{10,9},{11,1... | collective-permute-start | bytes 393224 | tf_op jit(solution)/shard_map/ppermute | solution.py:15
  183.2 1.5 copy-start.11
  189.6 1.6 copy-start.1
  189.6 1.6 copy-start.12
  196.1 1.5 copy-start.9
Sparse Core Ops, SparseCore 0:
  136.8 106.5 all-reduce.4
  246.2 269.1 all-reduce.6
